TPU v7x, 32 devices: a whole 2x2x4 slice. The times are simulated.
32 devices in a mesh: grp: 2 (over x), slab: 16 (over z, y, core).
Axes of the slice: x: 2, y: 2, z: 4, core: 2. Of those that a mesh axis runs over, the one named last changes fastest.
Arguments:
- right_side: bfloat16 [16, 12288, 128], P('grp', 'slab'), parts along dimension 0, may hold values from -6 to 6
- coupling: bfloat16 [96, 5, 2, 256, 128], P(('grp', 'slab')), parts along dimension 0, may hold values from -0.625 to 0.625
- diag_inverse: bfloat16 [96, 2, 256, 256], P(('grp', 'slab')), parts along dimension 0, may hold values from -0.125 to 0.125
- basis: bfloat16 [32, 2, 64, 256], P(('grp', 'slab')), parts along dimension 0, may hold values from -0.25 to 0.25
- near_tiles: int32 [48, 5], P('slab'), may hold values from 0 to 5, all different within a row
- far_basis: int32 [48, 2], P('slab'), may hold values from 0 to 15
Outputs:
- solution: bfloat16 [16, 12288, 128], P('grp', 'slab'), parts along dimension 0
There are 2 independent parts, one for each index of `grp`. A program takes and returns all parts, laid end to end along the dimension named above; an argument that names none is the same for every part. Nothing has to cross between parts.
Inputs may be any that keep to these rules, and one draw needn't show every extreme that they name: `near_tiles`: each row names 5 different tiles.
All inputs are finite; a program needn't handle non-finite values.
Results may differ from a plain program's by a relative error of at most 0.038.
Values may be sent and summed in bfloat16 or wider, within the bound.
A program may use at most 64 MiB of HBM per device.

v0:
```python
import jax
import jax.numpy as jnp
from jax import lax
from jax.sharding import PartitionSpec as P

BAND = 32


def from_behind(shard, axis, by):
    devices = lax.axis_size(axis)
    pairs = [(i, i + by) for i in range(devices) if 0 <= i + by < devices]
    return lax.ppermute(shard, axis, pairs)


def rotate(values):
    half_cols = values.shape[-1] // 2
    return jnp.concatenate([-values[..., half_cols:], values[..., :half_cols]], axis=-1)


def paired(values, position):
    return jnp.stack([values, rotate(values)], axis=position)


def body(right_side, coupling, diag_inverse, basis, near_tiles, far_basis):
    blocks = coupling.shape[0]
    block_rows = coupling.shape[3]
    tile_rows = coupling.shape[4]
    ticks, slab_rows, columns = right_side.shape
    rank_size = basis.shape[2]
    slabs = lax.axis_size("slab")
    myself = lax.axis_index("slab")
    offsets = jnp.arange(block_rows)[:, None] - jnp.arange(block_rows)[None, :]
    inside = jnp.abs(offsets) <= BAND
    banded = jnp.where(inside, diag_inverse, jnp.zeros_like(diag_inverse))
    gathered = lax.all_gather(basis, "slab", axis=0, tiled=True)
    picked = jnp.take(gathered, far_basis, axis=0)
    group = 1
    groups = ticks // group
    far_scale = 1.0 / jnp.sqrt((blocks * jnp.maximum(myself, 1)).astype(jnp.float32))

    def solve_group(panel, accum, slab_side):
        previous = panel.reshape(group, slab_rows // tile_rows, tile_rows, columns)
        chosen = previous[:, near_tiles]
        near_term = jnp.einsum(
            "bnprt,gbnptc->gbrc", coupling, paired(chosen, 3), preferred_element_type=jnp.float32
        )
        far_field = accum.astype(jnp.bfloat16)
        far_term = (
            jnp.einsum(
                "bpkr,gpkc->gbrc",
                picked[:, 1],
                paired(far_field, 1),
                preferred_element_type=jnp.float32,
            )
            * far_scale
        )
        modified = (
            slab_side.reshape(group, blocks, block_rows, columns).astype(jnp.float32)
            - near_term
            - far_term
        ).astype(jnp.bfloat16)
        solved = jnp.einsum(
            "bprs,gbpsc->gbrc", banded, paired(modified, 2), preferred_element_type=jnp.float32
        ).astype(jnp.bfloat16)
        coefficients = jnp.einsum(
            "bpkr,gbprc->gkc", picked[:, 0], paired(solved, 2), preferred_element_type=jnp.float32
        )
        return (solved.reshape(group, slab_rows, columns), accum + coefficients)

    def skipped(panel, accum, slab_side):
        return (jnp.zeros_like(panel), jnp.zeros_like(accum))

    def advance(turn, state):
        solved_all, panel, accum = state
        group_index = turn - myself
        active = jnp.logical_and(group_index >= 0, group_index < groups)
        first = jnp.clip(group_index, 0, groups - 1) * group
        slab_side = lax.dynamic_slice_in_dim(right_side, first, group, 0)
        solved, summed = lax.cond(active, solve_group, skipped, panel, accum, slab_side)
        current = lax.dynamic_slice_in_dim(solved_all, first, group, 0)
        solved_all = lax.dynamic_update_slice_in_dim(
            solved_all, jnp.where(active, solved, current), first, 0
        )
        panel = from_behind(solved, "slab", 1)
        accum = from_behind(summed.astype(jnp.bfloat16), "slab", 1).astype(summed.dtype)
        return (solved_all, panel, accum)

    start_state = (
        jnp.zeros((ticks, slab_rows, columns), jnp.bfloat16),
        jnp.zeros((group, slab_rows, columns), jnp.bfloat16),
        jnp.zeros((group, rank_size, columns), jnp.float32),
    )
    final_state = lax.fori_loop(0, slabs + groups - 1, advance, start_state)
    return final_state[0]


def solution(mesh):
    placed = (
        P("grp", "slab", None),
        P(("grp", "slab"), None, None, None, None),
        P(("grp", "slab"), None, None, None),
        P(("grp", "slab"), None, None, None),
        P("slab", None),
        P("slab", None),
    )
    return jax.shard_map(
        body, mesh=mesh, in_specs=placed, out_specs=P("grp", "slab", None), check_vma=False
    )
```

profile of v0, /device:TPU:29, one launch (start us, length us, event | category | flops | bytes accessed | tf_op | source)
XLA Modules:
  0.0 354.2 jit_solution(4081499192578733324)
XLA Ops:
  10.9 35.8 %all-gather.2.cloned.1.call-done = bf16[16,2,64,256]{3,2,1,0:T(8,128)(2,1)} async-done(((bf16[1,2,64,256]{3,2,1,0:T(8,128)(2,1)}), bf16[16,2,64,256]{3,2,1,0:T(8,128)(2,1)}) %all-gather.2.cloned.1.call-update) | async-done | bytes 1048592 | tf_op jit(solution)/shard_map/all_gather | solution.py:35
  50.1 297.2 %while.18 = (s32[]{:T(128)}, bf16[8,768,128]{2,1,0:T(8,128)(2,1)}, bf16[1,768,128]{2,1,0:T(8,128)(2,1)S(1)}, f32[1,64,128]{2,1,0:T(8,128)S(1)}, s32[]{:T(128)}, ...) while((s32[]{:T(128)}, bf16[8,768,128]{2,1,0:T(8,128)(2,1)}, ...), condition=%wide.region_3.4_spmd.clone, body=%wide.region_0.0_spmd.clone.sunk | while | flops 406271040 | bytes 16585984 | solution.py:93
  103.8 3.8 %collective-permute-done.1 = bf16[1,64,128]{2,1,0:T(8,128)(2,1)S(1)} collective-permute-done((bf16[1,64,128]{2,1,0:T(8,128)(2,1)S(1)}, bf16[1,64,128]{2,1,0:T(8,128)(2,1)S(1)}, u32[]{:S(2)}, u32[]{:S(2)}) %collective-permute-start.1) | collective-permute-done | bytes 16416 | tf_op jit(solution)/shard_map/while/body/eval_jaxpr/ppermute | solution.py:12
  112.0 3.8 %collective-permute-done.1 = bf16[1,64,128]{2,1,0:T(8,128)(2,1)S(1)} collective-permute-done((bf16[1,64,128]{2,1,0:T(8,128)(2,1)S(1)}, bf16[1,64,128]{2,1,0:T(8,128)(2,1)S(1)}, u32[]{:S(2)}, u32[]{:S(2)}) %collective-permute-start.1) | collective-permute-done | bytes 16416 | tf_op jit(solution)/shard_map/while/body/eval_jaxpr/ppermute | solution.py:12
  120.2 3.8 %collective-permute-done.1 = bf16[1,64,128]{2,1,0:T(8,128)(2,1)S(1)} collective-permute-done((bf16[1,64,128]{2,1,0:T(8,128)(2,1)S(1)}, bf16[1,64,128]{2,1,0:T(8,128)(2,1)S(1)}, u32[]{:S(2)}, u32[]{:S(2)}) %collective-permute-start.1) | collective-permute-done | bytes 16416 | tf_op jit(solution)/shard_map/while/body/eval_jaxpr/ppermute | solution.py:12
  128.3 3.8 %collective-permute-done.1 = bf16[1,64,128]{2,1,0:T(8,128)(2,1)S(1)} collective-permute-done((bf16[1,64,128]{2,1,0:T(8,128)(2,1)S(1)}, bf16[1,64,128]{2,1,0:T(8,128)(2,1)S(1)}, u32[]{:S(2)}, u32[]{:S(2)}) %collective-permute-start.1) | collective-permute-done | bytes 16416 | tf_op jit(solution)/shard_map/while/body/eval_jaxpr/ppermute | solution.py:12
  136.5 3.8 %collective-permute-done.1 = bf16[1,64,128]{2,1,0:T(8,128)(2,1)S(1)} collective-permute-done((bf16[1,64,128]{2,1,0:T(8,128)(2,1)S(1)}, bf16[1,64,128]{2,1,0:T(8,128)(2,1)S(1)}, u32[]{:S(2)}, u32[]{:S(2)}) %collective-permute-start.1) | collective-permute-done | bytes 16416 | tf_op jit(solution)/shard_map/while/body/eval_jaxpr/ppermute | solution.py:12
  144.7 3.8 %collective-permute-done.1 = bf16[1,64,128]{2,1,0:T(8,128)(2,1)S(1)} collective-permute-done((bf16[1,64,128]{2,1,0:T(8,128)(2,1)S(1)}, bf16[1,64,128]{2,1,0:T(8,128)(2,1)S(1)}, u32[]{:S(2)}, u32[]{:S(2)}) %collective-permute-start.1) | collective-permute-done | bytes 16416 | tf_op jit(solution)/shard_map/while/body/eval_jaxpr/ppermute | solution.py:12
  152.9 3.8 %collective-permute-done.1 = bf16[1,64,128]{2,1,0:T(8,128)(2,1)S(1)} collective-permute-done((bf16[1,64,128]{2,1,0:T(8,128)(2,1)S(1)}, bf16[1,64,128]{2,1,0:T(8,128)(2,1)S(1)}, u32[]{:S(2)}, u32[]{:S(2)}) %collective-permute-start.1) | collective-permute-done | bytes 16416 | tf_op jit(solution)/shard_map/while/body/eval_jaxpr/ppermute | solution.py:12
  161.0 71.5 %collective-permute-done.1 = bf16[1,64,128]{2,1,0:T(8,128)(2,1)S(1)} collective-permute-done((bf16[1,64,128]{2,1,0:T(8,128)(2,1)S(1)}, bf16[1,64,128]{2,1,0:T(8,128)(2,1)S(1)}, u32[]{:S(2)}, u32[]{:S(2)}) %collective-permute-start.1) | collective-permute-done | bytes 16416 | tf_op jit(solution)/shard_map/while/body/eval_jaxpr/ppermute | solution.py:12
  232.6 6.6 %conditional.3 = (bf16[1,768,128]{2,1,0:T(8,128)(2,1)S(1)}, bf16[1,64,128]{2,1,0:T(8,128)(2,1)S(1)}) conditional(s32[]{:T(128)} %convert_element_type.70, () %tuple.56, (bf16[8,768,128]{2,1,0:T(8,128)(2,1)}, s32[]{:T(128)}, bf16[1,768,128]{2,1,0:T(8,128)(2,1)S(1)}, s32[3,5]{1,0:T(4,128)S(1)}, bf16[3,5,2,256,128]{4,3,2,0,1:T(8,128)(2,1)}, ...), branch_computations={%region_1.1_spmd, %region_2.2_spmd.clone} | conditional | flops 406164544 | bytes 15094156 | solution.py:79
  243.4 3.8 %collective-permute-done.1 = bf16[1,64,128]{2,1,0:T(8,128)(2,1)S(1)} collective-permute-done((bf16[1,64,128]{2,1,0:T(8,128)(2,1)S(1)}, bf16[1,64,128]{2,1,0:T(8,128)(2,1)S(1)}, u32[]{:S(2)}, u32[]{:S(2)}) %collective-permute-start.1) | collective-permute-done | bytes 16416 | tf_op jit(solution)/shard_map/while/body/eval_jaxpr/ppermute | solution.py:12
  247.3 6.6 %conditional.3 = (bf16[1,768,128]{2,1,0:T(8,128)(2,1)S(1)}, bf16[1,64,128]{2,1,0:T(8,128)(2,1)S(1)}) conditional(s32[]{:T(128)} %convert_element_type.70, () %tuple.56, (bf16[8,768,128]{2,1,0:T(8,128)(2,1)}, s32[]{:T(128)}, bf16[1,768,128]{2,1,0:T(8,128)(2,1)S(1)}, s32[3,5]{1,0:T(4,128)S(1)}, bf16[3,5,2,256,128]{4,3,2,0,1:T(8,128)(2,1)}, ...), branch_computations={%region_1.1_spmd, %region_2.2_spmd.clone} | conditional | flops 406164544 | bytes 15094156 | solution.py:79
  258.2 3.8 %collective-permute-done.1 = bf16[1,64,128]{2,1,0:T(8,128)(2,1)S(1)} collective-permute-done((bf16[1,64,128]{2,1,0:T(8,128)(2,1)S(1)}, bf16[1,64,128]{2,1,0:T(8,128)(2,1)S(1)}, u32[]{:S(2)}, u32[]{:S(2)}) %collective-permute-start.1) | collective-permute-done | bytes 16416 | tf_op jit(solution)/shard_map/while/body/eval_jaxpr/ppermute | solution.py:12
  262.0 6.6 %conditional.3 = (bf16[1,768,128]{2,1,0:T(8,128)(2,1)S(1)}, bf16[1,64,128]{2,1,0:T(8,128)(2,1)S(1)}) conditional(s32[]{:T(128)} %convert_element_type.70, () %tuple.56, (bf16[8,768,128]{2,1,0:T(8,128)(2,1)}, s32[]{:T(128)}, bf16[1,768,128]{2,1,0:T(8,128)(2,1)S(1)}, s32[3,5]{1,0:T(4,128)S(1)}, bf16[3,5,2,256,128]{4,3,2,0,1:T(8,128)(2,1)}, ...), branch_computations={%region_1.1_spmd, %region_2.2_spmd.clone} | conditional | flops 406164544 | bytes 15094156 | solution.py:79
  272.9 3.8 %collective-permute-done.1 = bf16[1,64,128]{2,1,0:T(8,128)(2,1)S(1)} collective-permute-done((bf16[1,64,128]{2,1,0:T(8,128)(2,1)S(1)}, bf16[1,64,128]{2,1,0:T(8,128)(2,1)S(1)}, u32[]{:S(2)}, u32[]{:S(2)}) %collective-permute-start.1) | collective-permute-done | bytes 16416 | tf_op jit(solution)/shard_map/while/body/eval_jaxpr/ppermute | solution.py:12
  276.7 6.6 %conditional.3 = (bf16[1,768,128]{2,1,0:T(8,128)(2,1)S(1)}, bf16[1,64,128]{2,1,0:T(8,128)(2,1)S(1)}) conditional(s32[]{:T(128)} %convert_element_type.70, () %tuple.56, (bf16[8,768,128]{2,1,0:T(8,128)(2,1)}, s32[]{:T(128)}, bf16[1,768,128]{2,1,0:T(8,128)(2,1)S(1)}, s32[3,5]{1,0:T(4,128)S(1)}, bf16[3,5,2,256,128]{4,3,2,0,1:T(8,128)(2,1)}, ...), branch_computations={%region_1.1_spmd, %region_2.2_spmd.clone} | conditional | flops 406164544 | bytes 15094156 | solution.py:79
  287.6 3.8 %collective-permute-done.1 = bf16[1,64,128]{2,1,0:T(8,128)(2,1)S(1)} collective-permute-done((bf16[1,64,128]{2,1,0:T(8,128)(2,1)S(1)}, bf16[1,64,128]{2,1,0:T(8,128)(2,1)S(1)}, u32[]{:S(2)}, u32[]{:S(2)}) %collective-permute-start.1) | collective-permute-done | bytes 16416 | tf_op jit(solution)/shard_map/while/body/eval_jaxpr/ppermute | solution.py:12
  291.5 6.6 %conditional.3 = (bf16[1,768,128]{2,1,0:T(8,128)(2,1)S(1)}, bf16[1,64,128]{2,1,0:T(8,128)(2,1)S(1)}) conditional(s32[]{:T(128)} %convert_element_type.70, () %tuple.56, (bf16[8,768,128]{2,1,0:T(8,128)(2,1)}, s32[]{:T(128)}, bf16[1,768,128]{2,1,0:T(8,128)(2,1)S(1)}, s32[3,5]{1,0:T(4,128)S(1)}, bf16[3,5,2,256,128]{4,3,2,0,1:T(8,128)(2,1)}, ...), branch_computations={%region_1.1_spmd, %region_2.2_spmd.clone} | conditional | flops 406164544 | bytes 15094156 | solution.py:79
  302.4 3.8 %collective-permute-done.1 = bf16[1,64,128]{2,1,0:T(8,128)(2,1)S(1)} collective-permute-done((bf16[1,64,128]{2,1,0:T(8,128)(2,1)S(1)}, bf16[1,64,128]{2,1,0:T(8,128)(2,1)S(1)}, u32[]{:S(2)}, u32[]{:S(2)}) %collective-permute-start.1) | collective-permute-done | bytes 16416 | tf_op jit(solution)/shard_map/while/body/eval_jaxpr/ppermute | solution.py:12
  306.2 6.6 %conditional.3 = (bf16[1,768,128]{2,1,0:T(8,128)(2,1)S(1)}, bf16[1,64,128]{2,1,0:T(8,128)(2,1)S(1)}) conditional(s32[]{:T(128)} %convert_element_type.70, () %tuple.56, (bf16[8,768,128]{2,1,0:T(8,128)(2,1)}, s32[]{:T(128)}, bf16[1,768,128]{2,1,0:T(8,128)(2,1)S(1)}, s32[3,5]{1,0:T(4,128)S(1)}, bf16[3,5,2,256,128]{4,3,2,0,1:T(8,128)(2,1)}, ...), branch_computations={%region_1.1_spmd, %region_2.2_spmd.clone} | conditional | flops 406164544 | bytes 15094156 | solution.py:79
  317.1 3.8 %collective-permute-done.1 = bf16[1,64,128]{2,1,0:T(8,128)(2,1)S(1)} collective-permute-done((bf16[1,64,128]{2,1,0:T(8,128)(2,1)S(1)}, bf16[1,64,128]{2,1,0:T(8,128)(2,1)S(1)}, u32[]{:S(2)}, u32[]{:S(2)}) %collective-permute-start.1) | collective-permute-done | bytes 16416 | tf_op jit(solution)/shard_map/while/body/eval_jaxpr/ppermute | solution.py:12
  320.9 6.6 %conditional.3 = (bf16[1,768,128]{2,1,0:T(8,128)(2,1)S(1)}, bf16[1,64,128]{2,1,0:T(8,128)(2,1)S(1)}) conditional(s32[]{:T(128)} %convert_element_type.70, () %tuple.56, (bf16[8,768,128]{2,1,0:T(8,128)(2,1)}, s32[]{:T(128)}, bf16[1,768,128]{2,1,0:T(8,128)(2,1)S(1)}, s32[3,5]{1,0:T(4,128)S(1)}, bf16[3,5,2,256,128]{4,3,2,0,1:T(8,128)(2,1)}, ...), branch_computations={%region_1.1_spmd, %region_2.2_spmd.clone} | conditional | flops 406164544 | bytes 15094156 | solution.py:79
  335.7 6.6 %conditional.3 = (bf16[1,768,128]{2,1,0:T(8,128)(2,1)S(1)}, bf16[1,64,128]{2,1,0:T(8,128)(2,1)S(1)}) conditional(s32[]{:T(128)} %convert_element_type.70, () %tuple.56, (bf16[8,768,128]{2,1,0:T(8,128)(2,1)}, s32[]{:T(128)}, bf16[1,768,128]{2,1,0:T(8,128)(2,1)S(1)}, s32[3,5]{1,0:T(4,128)S(1)}, bf16[3,5,2,256,128]{4,3,2,0,1:T(8,128)(2,1)}, ...), branch_computations={%region_1.1_spmd, %region_2.2_spmd.clone} | conditional | flops 406164544 | bytes 15094156 | solution.py:79
  (392 shorter events, 181.9 us)
Async XLA Ops:
  6.5 40.2 %all-gather.2.cloned.1.call-start = ((), (), s32[]{:S(2)}) async-start(), calls=%async_computation | async-start | bytes 1114112 | tf_op jit(solution)/shard_map/all_gather | solution.py:35
  55.3 7.0 %collective-permute-start = (bf16[1,768,128]{2,1,0:T(8,128)(2,1)S(1)}, bf16[1,768,128]{2,1,0:T(8,128)(2,1)S(1)}, u32[]{:S(2)}, u32[]{:S(2)}) collective-permute-start(bf16[1,768,128]{2,1,0:T(8,128)(2,1)S(1)} %get-tuple-element.438), channel_id=1, source_target_pairs={{0,1},{1,2},{2,3},{3,4},{4,5},{5,6},{6,7},{7,8},{8,9},{9,10},{10,1... | collective-permute-start | bytes 589832 | tf_op jit(solution)/shard_map/while/body/eval_jaxpr/ppermute | solution.py:12
  62.4 7.2 %collective-permute-start = (bf16[1,768,128]{2,1,0:T(8,128)(2,1)S(1)}, bf16[1,768,128]{2,1,0:T(8,128)(2,1)S(1)}, u32[]{:S(2)}, u32[]{:S(2)}) collective-permute-start(bf16[1,768,128]{2,1,0:T(8,128)(2,1)S(1)} %get-tuple-element.438), channel_id=1, source_target_pairs={{0,1},{1,2},{2,3},{3,4},{4,5},{5,6},{6,7},{7,8},{8,9},{9,10},{10,1... | collective-permute-start | bytes 589832 | tf_op jit(solution)/shard_map/while/body/eval_jaxpr/ppermute | solution.py:12
  69.7 7.2 %collective-permute-start = (bf16[1,768,128]{2,1,0:T(8,128)(2,1)S(1)}, bf16[1,768,128]{2,1,0:T(8,128)(2,1)S(1)}, u32[]{:S(2)}, u32[]{:S(2)}) collective-permute-start(bf16[1,768,128]{2,1,0:T(8,128)(2,1)S(1)} %get-tuple-element.438), channel_id=1, source_target_pairs={{0,1},{1,2},{2,3},{3,4},{4,5},{5,6},{6,7},{7,8},{8,9},{9,10},{10,1... | collective-permute-start | bytes 589832 | tf_op jit(solution)/shard_map/while/body/eval_jaxpr/ppermute | solution.py:12
  77.0 7.2 %collective-permute-start = (bf16[1,768,128]{2,1,0:T(8,128)(2,1)S(1)}, bf16[1,768,128]{2,1,0:T(8,128)(2,1)S(1)}, u32[]{:S(2)}, u32[]{:S(2)}) collective-permute-start(bf16[1,768,128]{2,1,0:T(8,128)(2,1)S(1)} %get-tuple-element.438), channel_id=1, source_target_pairs={{0,1},{1,2},{2,3},{3,4},{4,5},{5,6},{6,7},{7,8},{8,9},{9,10},{10,1... | collective-permute-start | bytes 589832 | tf_op jit(solution)/shard_map/while/body/eval_jaxpr/ppermute | solution.py:12
  84.2 7.2 %collective-permute-start = (bf16[1,768,128]{2,1,0:T(8,128)(2,1)S(1)}, bf16[1,768,128]{2,1,0:T(8,128)(2,1)S(1)}, u32[]{:S(2)}, u32[]{:S(2)}) collective-permute-start(bf16[1,768,128]{2,1,0:T(8,128)(2,1)S(1)} %get-tuple-element.438), channel_id=1, source_target_pairs={{0,1},{1,2},{2,3},{3,4},{4,5},{5,6},{6,7},{7,8},{8,9},{9,10},{10,1... | collective-permute-start | bytes 589832 | tf_op jit(solution)/shard_map/while/body/eval_jaxpr/ppermute | solution.py:12
  91.5 8.0 %collective-permute-start = (bf16[1,768,128]{2,1,0:T(8,128)(2,1)S(1)}, bf16[1,768,128]{2,1,0:T(8,128)(2,1)S(1)}, u32[]{:S(2)}, u32[]{:S(2)}) collective-permute-start(bf16[1,768,128]{2,1,0:T(8,128)(2,1)S(1)} %get-tuple-element.438), channel_id=1, source_target_pairs={{0,1},{1,2},{2,3},{3,4},{4,5},{5,6},{6,7},{7,8},{8,9},{9,10},{10,1... | collective-permute-start | bytes 589832 | tf_op jit(solution)/shard_map/while/body/eval_jaxpr/ppermute | solution.py:12
  99.6 8.1 %collective-permute-start = (bf16[1,768,128]{2,1,0:T(8,128)(2,1)S(1)}, bf16[1,768,128]{2,1,0:T(8,128)(2,1)S(1)}, u32[]{:S(2)}, u32[]{:S(2)}) collective-permute-start(bf16[1,768,128]{2,1,0:T(8,128)(2,1)S(1)} %get-tuple-element.438), channel_id=1, source_target_pairs={{0,1},{1,2},{2,3},{3,4},{4,5},{5,6},{6,7},{7,8},{8,9},{9,10},{10,1... | collective-permute-start | bytes 589832 | tf_op jit(solution)/shard_map/while/body/eval_jaxpr/ppermute | solution.py:12
  107.7 8.1 %collective-permute-start = (bf16[1,768,128]{2,1,0:T(8,128)(2,1)S(1)}, bf16[1,768,128]{2,1,0:T(8,128)(2,1)S(1)}, u32[]{:S(2)}, u32[]{:S(2)}) collective-permute-start(bf16[1,768,128]{2,1,0:T(8,128)(2,1)S(1)} %get-tuple-element.438), channel_id=1, source_target_pairs={{0,1},{1,2},{2,3},{3,4},{4,5},{5,6},{6,7},{7,8},{8,9},{9,10},{10,1... | collective-permute-start | bytes 589832 | tf_op jit(solution)/shard_map/while/body/eval_jaxpr/ppermute | solution.py:12
  115.9 8.1 %collective-permute-start = (bf16[1,768,128]{2,1,0:T(8,128)(2,1)S(1)}, bf16[1,768,128]{2,1,0:T(8,128)(2,1)S(1)}, u32[]{:S(2)}, u32[]{:S(2)}) collective-permute-start(bf16[1,768,128]{2,1,0:T(8,128)(2,1)S(1)} %get-tuple-element.438), channel_id=1, source_target_pairs={{0,1},{1,2},{2,3},{3,4},{4,5},{5,6},{6,7},{7,8},{8,9},{9,10},{10,1... | collective-permute-start | bytes 589832 | tf_op jit(solution)/shard_map/while/body/eval_jaxpr/ppermute | solution.py:12
  124.1 8.1 %collective-permute-start = (bf16[1,768,128]{2,1,0:T(8,128)(2,1)S(1)}, bf16[1,768,128]{2,1,0:T(8,128)(2,1)S(1)}, u32[]{:S(2)}, u32[]{:S(2)}) collective-permute-start(bf16[1,768,128]{2,1,0:T(8,128)(2,1)S(1)} %get-tuple-element.438), channel_id=1, source_target_pairs={{0,1},{1,2},{2,3},{3,4},{4,5},{5,6},{6,7},{7,8},{8,9},{9,10},{10,1... | collective-permute-start | bytes 589832 | tf_op jit(solution)/shard_map/while/body/eval_jaxpr/ppermute | solution.py:12
  132.2 8.1 %collective-permute-start = (bf16[1,768,128]{2,1,0:T(8,128)(2,1)S(1)}, bf16[1,768,128]{2,1,0:T(8,128)(2,1)S(1)}, u32[]{:S(2)}, u32[]{:S(2)}) collective-permute-start(bf16[1,768,128]{2,1,0:T(8,128)(2,1)S(1)} %get-tuple-element.438), channel_id=1, source_target_pairs={{0,1},{1,2},{2,3},{3,4},{4,5},{5,6},{6,7},{7,8},{8,9},{9,10},{10,1... | collective-permute-start | bytes 589832 | tf_op jit(solution)/shard_map/while/body/eval_jaxpr/ppermute | solution.py:12
  140.4 8.1 %collective-permute-start = (bf16[1,768,128]{2,1,0:T(8,128)(2,1)S(1)}, bf16[1,768,128]{2,1,0:T(8,128)(2,1)S(1)}, u32[]{:S(2)}, u32[]{:S(2)}) collective-permute-start(bf16[1,768,128]{2,1,0:T(8,128)(2,1)S(1)} %get-tuple-element.438), channel_id=1, source_target_pairs={{0,1},{1,2},{2,3},{3,4},{4,5},{5,6},{6,7},{7,8},{8,9},{9,10},{10,1... | collective-permute-start | bytes 589832 | tf_op jit(solution)/shard_map/while/body/eval_jaxpr/ppermute | solution.py:12
  148.6 8.1 %collective-permute-start = (bf16[1,768,128]{2,1,0:T(8,128)(2,1)S(1)}, bf16[1,768,128]{2,1,0:T(8,128)(2,1)S(1)}, u32[]{:S(2)}, u32[]{:S(2)}) collective-permute-start(bf16[1,768,128]{2,1,0:T(8,128)(2,1)S(1)} %get-tuple-element.438), channel_id=1, source_target_pairs={{0,1},{1,2},{2,3},{3,4},{4,5},{5,6},{6,7},{7,8},{8,9},{9,10},{10,1... | collective-permute-start | bytes 589832 | tf_op jit(solution)/shard_map/while/body/eval_jaxpr/ppermute | solution.py:12
  149.9 6.8 %collective-permute-start.1 = (bf16[1,64,128]{2,1,0:T(8,128)(2,1)S(1)}, bf16[1,64,128]{2,1,0:T(8,128)(2,1)S(1)}, u32[]{:S(2)}, u32[]{:S(2)}) collective-permute-start(bf16[1,64,128]{2,1,0:T(8,128)(2,1)S(1)} %get-tuple-element.439), channel_id=1, source_target_pairs={{0,1},{1,2},{2,3},{3,4},{4,5},{5,6},{6,7},{7,8},{8,9},{9,10},{10,1... | collective-permute-start | bytes 49160 | tf_op jit(solution)/shard_map/while/body/eval_jaxpr/ppermute | solution.py:12
  156.8 75.8 %collective-permute-start = (bf16[1,768,128]{2,1,0:T(8,128)(2,1)S(1)}, bf16[1,768,128]{2,1,0:T(8,128)(2,1)S(1)}, u32[]{:S(2)}, u32[]{:S(2)}) collective-permute-start(bf16[1,768,128]{2,1,0:T(8,128)(2,1)S(1)} %get-tuple-element.438), channel_id=1, source_target_pairs={{0,1},{1,2},{2,3},{3,4},{4,5},{5,6},{6,7},{7,8},{8,9},{9,10},{10,1... | collective-permute-start | bytes 589832 | tf_op jit(solution)/shard_map/while/body/eval_jaxpr/ppermute | solution.py:12
  158.1 74.5 %collective-permute-start.1 = (bf16[1,64,128]{2,1,0:T(8,128)(2,1)S(1)}, bf16[1,64,128]{2,1,0:T(8,128)(2,1)S(1)}, u32[]{:S(2)}, u32[]{:S(2)}) collective-permute-start(bf16[1,64,128]{2,1,0:T(8,128)(2,1)S(1)} %get-tuple-element.439), channel_id=1, source_target_pairs={{0,1},{1,2},{2,3},{3,4},{4,5},{5,6},{6,7},{7,8},{8,9},{9,10},{10,1... | collective-permute-start | bytes 49160 | tf_op jit(solution)/shard_map/while/body/eval_jaxpr/ppermute | solution.py:12
  239.2 8.1 %collective-permute-start = (bf16[1,768,128]{2,1,0:T(8,128)(2,1)S(1)}, bf16[1,768,128]{2,1,0:T(8,128)(2,1)S(1)}, u32[]{:S(2)}, u32[]{:S(2)}) collective-permute-start(bf16[1,768,128]{2,1,0:T(8,128)(2,1)S(1)} %get-tuple-element.438), channel_id=1, source_target_pairs={{0,1},{1,2},{2,3},{3,4},{4,5},{5,6},{6,7},{7,8},{8,9},{9,10},{10,1... | collective-permute-start | bytes 589832 | tf_op jit(solution)/shard_map/while/body/eval_jaxpr/ppermute | solution.py:12
  253.9 8.1 %collective-permute-start = (bf16[1,768,128]{2,1,0:T(8,128)(2,1)S(1)}, bf16[1,768,128]{2,1,0:T(8,128)(2,1)S(1)}, u32[]{:S(2)}, u32[]{:S(2)}) collective-permute-start(bf16[1,768,128]{2,1,0:T(8,128)(2,1)S(1)} %get-tuple-element.438), channel_id=1, source_target_pairs={{0,1},{1,2},{2,3},{3,4},{4,5},{5,6},{6,7},{7,8},{8,9},{9,10},{10,1... | collective-permute-start | bytes 589832 | tf_op jit(solution)/shard_map/while/body/eval_jaxpr/ppermute | solution.py:12
  268.6 8.1 %collective-permute-start = (bf16[1,768,128]{2,1,0:T(8,128)(2,1)S(1)}, bf16[1,768,128]{2,1,0:T(8,128)(2,1)S(1)}, u32[]{:S(2)}, u32[]{:S(2)}) collective-permute-start(bf16[1,768,128]{2,1,0:T(8,128)(2,1)S(1)} %get-tuple-element.438), channel_id=1, source_target_pairs={{0,1},{1,2},{2,3},{3,4},{4,5},{5,6},{6,7},{7,8},{8,9},{9,10},{10,1... | collective-permute-start | bytes 589832 | tf_op jit(solution)/shard_map/while/body/eval_jaxpr/ppermute | solution.py:12
  283.4 8.1 %collective-permute-start = (bf16[1,768,128]{2,1,0:T(8,128)(2,1)S(1)}, bf16[1,768,128]{2,1,0:T(8,128)(2,1)S(1)}, u32[]{:S(2)}, u32[]{:S(2)}) collective-permute-start(bf16[1,768,128]{2,1,0:T(8,128)(2,1)S(1)} %get-tuple-element.438), channel_id=1, source_target_pairs={{0,1},{1,2},{2,3},{3,4},{4,5},{5,6},{6,7},{7,8},{8,9},{9,10},{10,1... | collective-permute-start | bytes 589832 | tf_op jit(solution)/shard_map/while/body/eval_jaxpr/ppermute | solution.py:12
  298.1 8.1 %collective-permute-start = (bf16[1,768,128]{2,1,0:T(8,128)(2,1)S(1)}, bf16[1,768,128]{2,1,0:T(8,128)(2,1)S(1)}, u32[]{:S(2)}, u32[]{:S(2)}) collective-permute-start(bf16[1,768,128]{2,1,0:T(8,128)(2,1)S(1)} %get-tuple-element.438), channel_id=1, source_target_pairs={{0,1},{1,2},{2,3},{3,4},{4,5},{5,6},{6,7},{7,8},{8,9},{9,10},{10,1... | collective-permute-start | bytes 589832 | tf_op jit(solution)/shard_map/while/body/eval_jaxpr/ppermute | solution.py:12
  312.8 8.1 %collective-permute-start = (bf16[1,768,128]{2,1,0:T(8,128)(2,1)S(1)}, bf16[1,768,128]{2,1,0:T(8,128)(2,1)S(1)}, u32[]{:S(2)}, u32[]{:S(2)}) collective-permute-start(bf16[1,768,128]{2,1,0:T(8,128)(2,1)S(1)} %get-tuple-element.438), channel_id=1, source_target_pairs={{0,1},{1,2},{2,3},{3,4},{4,5},{5,6},{6,7},{7,8},{8,9},{9,10},{10,1... | collective-permute-start | bytes 589832 | tf_op jit(solution)/shard_map/while/body/eval_jaxpr/ppermute | solution.py:12
  327.6 8.1 %collective-permute-start = (bf16[1,768,128]{2,1,0:T(8,128)(2,1)S(1)}, bf16[1,768,128]{2,1,0:T(8,128)(2,1)S(1)}, u32[]{:S(2)}, u32[]{:S(2)}) collective-permute-start(bf16[1,768,128]{2,1,0:T(8,128)(2,1)S(1)} %get-tuple-element.438), channel_id=1, source_target_pairs={{0,1},{1,2},{2,3},{3,4},{4,5},{5,6},{6,7},{7,8},{8,9},{9,10},{10,1... | collective-permute-start | bytes 589832 | tf_op jit(solution)/shard_map/while/body/eval_jaxpr/ppermute | solution.py:12
  (26 other events, 149.4 us)
Sparse Core Ops, SparseCore 0:
  9.5 37.2 all-gather.1
where the time goes:
time: 359 us; the launch traced here: 354 us
  waiting for transfers between devices  181 us (50%)
  starting transfers between devices  59.4 us (17%)
  other arithmetic  41.3 us (12%)
  local copies, waits for them, and re-layouts  30.4 us (8%)
  matrix products  25.8 us (7%)
  between operations  13.5 us (4%)
    ppermute x46, waiting for transfers between devices, from_behind(): return lax.ppermute(shard, axis, pairs)  144 us
    ppermute x46, starting transfers between devices, from_behind(): return lax.ppermute(shard, axis, pairs)  59.4 us
    dynamic_update_slice x23, other arithmetic, advance(): lax.dynamic_update_slice_in_dim(solved_all, jnp.where(active, solved, cur...  38.3 us
    all_gather x1, waiting for transfers between devices, body(): gathered = lax.all_gather(basis, 'slab', axis=0, tiled=True)  35.8 us
    dot_general x8, matrix products, solve_group(): jnp.einsum('bnprt,gbnptc->gbrc', coupling, paired(chosen, 3), preferred_e...  18.7 us
    dynamic_slice x8, local copies, waits for them, and re-layouts, advance(): slab_side = lax.dynamic_slice_in_dim(right_side, first, group, 0)  7.57 us
  transfers between devices with their start and end apart: 47, of which 24 were waited for; matrix products, arithmetic and copies ran while one was open for 12% of the time, Pallas kernels for 0%

commit v1 on v0

v1 whole, which is shorter than its diff:
```python
import functools

import jax
import jax.numpy as jnp
from jax import lax
from jax.experimental import pallas as pl
from jax.experimental.pallas import tpu as pltpu
from jax.sharding import PartitionSpec as P

BAND = 32
MESH = pl.DeviceIdType.MESH
F32 = jnp.float32
BF16 = jnp.bfloat16


def turned(values):
    half = values.shape[-1] // 2
    rolled = pltpu.roll(values, half, 1)
    lane = lax.broadcasted_iota(jnp.int32, values.shape, 1)
    return jnp.where(lane < half, -rolled, rolled)


def complex_sum(stacked):
    rows = stacked.shape[0] // 2
    return stacked[:rows] + turned(stacked[rows:])


def mul(a, b):
    return jnp.dot(a, b, preferred_element_type=F32)


def kernel(
    n, rs, cp, di, ba, nt, fb, scale, out,
    gath, w, ds, bd, nn, y, vbuf, sbuf, gs, gr, cs, cr,
):
    blocks, near, _, blk, tile = cp.shape
    ticks, rows, _ = rs.shape
    rank = ba.shape[2]
    tiles = rows // tile
    two = 2 * blk
    me = lax.axis_index("slab")
    depth = n // 4
    z, q = me // 4, me % 4
    across = z * 4 + (q + 2) % 4
    beside = me + 1 - 2 * (q % 2)

    barrier = pltpu.get_barrier_semaphore()

    def greet(there, who):
        @pl.when(there)
        def _():
            pl.semaphore_signal(barrier, inc=1, device_id={"slab": who}, device_id_type=MESH)

    sides = (
        (me > 0, me - 1),
        (me < n - 1, me + 1),
        (z > 0, me - 4),
        (z < depth - 1, me + 4),
        (me >= 0, across),
    )
    for there, who in sides:
        greet(there, who)
    pl.semaphore_wait(barrier, sum(there.astype(jnp.int32) for there, _ in sides))

    def basis_copy(way, slot, who, own=False):
        return pltpu.make_async_remote_copy(
            src_ref=ba.at[0] if own else gath.at[slot],
            dst_ref=gath.at[slot],
            send_sem=gs.at[way, slot],
            recv_sem=gr.at[slot],
            device_id={"slab": who},
            device_id_type=MESH,
        )

    def arrived(slot):
        basis_copy(0, slot, beside).wait_recv()

    def own_out(finish):
        def one(there, way, who):
            @pl.when(there)
            def _():
                copy = basis_copy(way, me, who, own=True)
                copy.wait_send() if finish else copy.start()

        one(z < depth - 1, 0, me + 4)
        one(z > 0, 1, me - 4)
        one(me >= 0, 2, across)
        one(me >= 0, 3, beside)

    def line(k, finish):
        def one(there, way, who, slot):
            @pl.when(there)
            def _():
                copy = basis_copy(way, slot, who)
                copy.wait_send() if finish else copy.start()

        low, high = me - 4 * k, me + 4 * k

        @pl.when(z >= k)
        def _():
            if not finish:
                arrived(low)
            one(z < depth - 1, 0, me + 4, low)
            one(me >= 0, 2, across, low)
            one(me >= 0, 3, beside, low)

        @pl.when(z + k < depth)
        def _():
            if not finish:
                arrived(high)
            one(z > 0, 1, me - 4, high)
            one(me >= 0, 2, across, high)
            one(me >= 0, 3, beside, high)

    def other_line(k, finish):
        slot = k * 4 + (q + 2) % 4
        copy = basis_copy(3, slot, beside)
        if finish:
            copy.wait_send()
        else:
            arrived(slot)
            copy.start()

    def others_in(k):
        arrived(k * 4 + beside % 4)
        arrived(k * 4 + (beside + 2) % 4)

    own_out(False)
    gath[me] = ba[0]

    offset = lax.broadcasted_iota(jnp.int32, (blk, blk), 0) - lax.broadcasted_iota(
        jnp.int32, (blk, blk), 1
    )
    inside = jnp.abs(offset) <= BAND
    for b in range(blocks):
        for p in range(2):
            part = jnp.where(inside, di[b, p].astype(F32), 0.0)
            ds[b, p * blk : (p + 1) * blk, 0:blk] = part.astype(BF16)
            other = part if p == 0 else -part
            ds[b, (1 - p) * blk : (2 - p) * blk, blk:two] = other.astype(BF16)

    def near_block(b):
        for j in range(tiles):
            place, held = jnp.int32(0), jnp.int32(0)
            for m in range(near):
                hit = (nt[b, m] == j).astype(jnp.int32)
                place = jnp.maximum(place, m * hit)
                held = jnp.maximum(held, hit)
            keep = held.astype(F32)
            for p in range(2):
                piece = cp[b, place, p].astype(F32) * keep
                nn[p * blk : (p + 1) * blk, j * tile : (j + 1) * tile] = piece.astype(BF16)
        w[b * two : (b + 1) * two, 0:rows] = mul(ds[b], nn[...]).astype(BF16)

    near_block(0)
    for k in range(1, blocks):
        line(k, False)
        near_block(k)

    def line_loop(k, carry):
        line(k, False)
        return carry

    lax.fori_loop(blocks, depth, line_loop, 0)

    def other_loop(k, carry):
        other_line(k, False)
        return carry

    lax.fori_loop(0, depth, other_loop, 0)

    def side_tick(t, carry):
        for b in range(blocks):
            piece = rs[t, b * blk : (b + 1) * blk, :]
            y[t, b * blk : (b + 1) * blk, :] = complex_sum(mul(ds[b, :, 0:blk], piece))
        return carry

    lax.fori_loop(0, ticks, side_tick, 0)

    def others_loop(k, carry):
        others_in(k)
        return carry

    lax.fori_loop(0, depth, others_loop, 0)

    total = jnp.zeros((2 * rank, rows + rank), F32)
    for b in range(blocks):
        far = jnp.concatenate([gath[fb[b, 1], 0], gath[fb[b, 1], 1]], axis=1)
        spread = lax.dot_general(
            ds[b], far, (((1,), (1,)), ((), ())), preferred_element_type=F32
        )
        w[b * two : (b + 1) * two, rows : rows + rank] = (spread * scale[0]).astype(BF16)
        real, imag = gath[fb[b, 0], 0], gath[fb[b, 0], 1]
        both = jnp.concatenate(
            [
                jnp.concatenate([real, -imag], axis=1),
                jnp.concatenate([imag, real], axis=1),
            ],
            axis=0,
        )
        total = total + mul(both, w[b * two : (b + 1) * two, :])
        bd[b] = mul(both, ds[b, :, 0:blk]).astype(BF16)
    w[blocks * two : blocks * two + 2 * rank, :] = total.astype(BF16)

    def gain_tick(t, carry):
        gain = jnp.zeros((2 * rank, rs.shape[2]), F32)
        for b in range(blocks):
            gain = gain + mul(bd[b], rs[t, b * blk : (b + 1) * blk, :])
        y[t, rows : rows + rank, :] = complex_sum(gain)
        return carry

    lax.fori_loop(0, ticks, gain_tick, 0)

    @pl.when(me == 0)
    def _():
        vbuf[...] = jnp.zeros_like(vbuf)

    def chain_copy(t, c):
        first = c * blk
        count = blk if c < blocks else rank
        return pltpu.make_async_remote_copy(
            src_ref=sbuf.at[t, pl.ds(first, count)],
            dst_ref=vbuf.at[t, pl.ds(first, count)],
            send_sem=cs.at[t, c],
            recv_sem=cr.at[t, c],
            device_id={"slab": me + 1},
            device_id_type=MESH,
        )

    def tick(t, carry):
        @pl.when(me > 0)
        def _():
            for c in range(blocks + 1):
                chain_copy(t, c).wait_recv()

        state = vbuf[t]
        for b in range(blocks):
            part = slice(b * blk, (b + 1) * blk)
            solved = y[t, part, :] - complex_sum(mul(w[b * two : (b + 1) * two, :], state))
            solved = solved.astype(BF16)
            out[t, part, :] = solved
            sbuf[t, part, :] = solved

            @pl.when(me < n - 1)
            def _():
                chain_copy(t, b).start()

        part = slice(rows, rows + rank)
        gained = y[t, part, :] - complex_sum(mul(w[blocks * two :, :], state))
        sbuf[t, part, :] = (vbuf[t, part, :].astype(F32) + gained).astype(BF16)

        @pl.when(me < n - 1)
        def _():
            chain_copy(t, blocks).start()

        return carry

    lax.fori_loop(0, ticks, tick, 0)

    def chain_end(t, carry):
        for c in range(blocks + 1):
            chain_copy(t, c).wait_send()
        return carry

    @pl.when(me < n - 1)
    def _():
        lax.fori_loop(0, ticks, chain_end, 0)

    own_out(True)

    def line_end(k, carry):
        line(k, True)
        return carry

    lax.fori_loop(1, depth, line_end, 0)

    def other_end(k, carry):
        other_line(k, True)
        return carry

    lax.fori_loop(0, depth, other_end, 0)


def body(right_side, coupling, diag_inverse, basis, near_tiles, far_basis):
    blocks, _, _, blk, _ = coupling.shape
    ticks, rows, columns = right_side.shape
    rank = basis.shape[2]
    n = lax.axis_size("slab")
    earlier = blocks * jnp.maximum(lax.axis_index("slab"), 1)
    scale = (1.0 / jnp.sqrt(earlier.astype(F32))).reshape(1)
    vmem = pl.BlockSpec(memory_space=pltpu.VMEM)
    smem = pl.BlockSpec(memory_space=pltpu.SMEM)
    return pl.pallas_call(
        functools.partial(kernel, n),
        out_shape=jax.ShapeDtypeStruct(right_side.shape, right_side.dtype),
        in_specs=[vmem] * 4 + [smem] * 3,
        out_specs=vmem,
        scratch_shapes=[
            pltpu.VMEM((n,) + basis.shape[1:], BF16),
            pltpu.VMEM((2 * (rows + rank), rows + rank), BF16),
            pltpu.VMEM((blocks, 2 * blk, 2 * blk), BF16),
            pltpu.VMEM((blocks, 2 * rank, blk), BF16),
            pltpu.VMEM((2 * blk, rows), BF16),
            pltpu.VMEM((ticks, rows + rank, columns), F32),
            pltpu.VMEM((ticks, rows + rank, columns), BF16),
            pltpu.VMEM((ticks, rows + rank, columns), BF16),
            pltpu.SemaphoreType.DMA((4, n)),
            pltpu.SemaphoreType.DMA((n,)),
            pltpu.SemaphoreType.DMA((ticks, blocks + 1)),
            pltpu.SemaphoreType.DMA((ticks, blocks + 1)),
        ],
        compiler_params=pltpu.CompilerParams(
            collective_id=0, has_side_effects=True, vmem_limit_bytes=48 * 1024 * 1024
        ),
    )(right_side, coupling, diag_inverse, basis, near_tiles, far_basis, scale)


def solution(mesh):
    placed = (
        P("grp", "slab", None),
        P(("grp", "slab"), None, None, None, None),
        P(("grp", "slab"), None, None, None),
        P(("grp", "slab"), None, None, None),
        P("slab", None),
        P("slab", None),
    )
    return jax.shard_map(
        body, mesh=mesh, in_specs=placed, out_specs=P("grp", "slab", None), check_vma=False
    )
```

time: 359 us -> 110 us (0.31); the launches traced: 354 us -> 109 us
  waiting for transfers between devices: 181 us -> 0 us
  Pallas kernels: 0 us -> 102 us
  starting transfers between devices: 59.4 us -> 0 us
  other arithmetic: 41.3 us -> 0 us
  matrix products: 25.8 us -> 0 us
  local copies, waits for them, and re-layouts: 30.4 us -> 7.52 us
  between operations: 13.5 us -> 0.06 us
    ppermute x46 -> x0, waiting for transfers between devices: 144 us -> none  [from_behind(): return lax.ppermute(shard, axis, pairs)]
    pallas_call x0 -> x1, Pallas kernels: none -> 102 us  [body(): pl.pallas_call(functools.partial(kernel, n), out_shape=jax.ShapeDtypeStru...]
    ppermute x46 -> x0, starting transfers between devices: 59.4 us -> none  [from_behind(): return lax.ppermute(shard, axis, pairs)]
    dynamic_update_slice x23 -> x0, other arithmetic: 38.3 us -> none  [advance(): lax.dynamic_update_slice_in_dim(solved_all, jnp.where(active, solved, cur...]
    all_gather x1 -> x0, waiting for transfers between devices: 35.8 us -> none  [body(): gathered = lax.all_gather(basis, 'slab', axis=0, tiled=True)]
    dot_general x32 -> x0, matrix products: 25.8 us -> none  [the longest x8 18.7 us: solve_group(): jnp.einsum('bnprt,gbnptc->gbrc', coupling, paired(chosen, 3), preferred_e...]
    dynamic_slice x8 -> x0, local copies, waits for them, and re-layouts: 7.57 us -> none  [advance(): slab_side = lax.dynamic_slice_in_dim(right_side, first, group, 0)]
    gather x9 -> x0, local copies, waits for them, and re-layouts: 6.93 us -> none  [the longest x8 5.13 us: solve_group(): chosen = previous[:, near_tiles]]
  transfers between devices with their start and end apart: 47 -> 0, of which waited for: 24 -> 0; matrix products, arithmetic and copies ran while one was open for 12% -> 0% of each run, Pallas kernels for 0% -> 0%
where the time goes in v1:
time: 110 us; the launch traced here: 109 us
  Pallas kernels  102 us (93%)
  local copies, waits for them, and re-layouts  7.52 us (7%)
    pallas_call x1, Pallas kernels, body(): pl.pallas_call(functools.partial(kernel, n), out_shape=jax.ShapeDtypeStru...  102 us
    unnamed x12, local copies, waits for them, and re-layouts  7.52 us

profile of v1, /device:TPU:29, one launch (start us, length us, event | category | flops | bytes accessed | tf_op | source)
XLA Modules:
  0.0 109.3 jit_solution(3401081948111320874)
XLA Ops:
  0.0 0.8 copy.7.fb
  0.8 0.0 copy-start
  0.8 1.5 %copy-done = bf16[3,5,2,256,128]{4,3,2,1,0:T(8,128)(2,1)S(1)} copy-done((bf16[3,5,2,256,128]{4,3,2,1,0:T(8,128)(2,1)S(1)}, bf16[3,5,2,256,128]{4,3,2,1,0:T(8,128)(2,1)}, u32[]{:S(2)}) %copy-start) | copy-done | bytes 1966104
  2.4 0.0 copy-start.1
  2.4 1.4 %copy-done.1 = bf16[8,768,128]{2,1,0:T(8,128)(2,1)S(1)} copy-done((bf16[8,768,128]{2,1,0:T(8,128)(2,1)S(1)}, bf16[8,768,128]{2,1,0:T(8,128)(2,1)}, u32[]{:S(2)}) %copy-start.1) | copy-done | bytes 1572888
  3.8 0.0 copy-start.2
  3.8 1.1 %copy-done.2 = bf16[3,2,256,256]{3,2,1,0:T(8,128)(2,1)S(1)} copy-done((bf16[3,2,256,256]{3,2,1,0:T(8,128)(2,1)S(1)}, bf16[3,2,256,256]{3,2,1,0:T(8,128)(2,1)}, u32[]{:S(2)}) %copy-start.2) | copy-done | bytes 786456
  4.9 0.0 copy-start.3
  4.9 0.8 copy-done.3
  5.7 0.0 copy-start.4
  5.7 0.7 copy-done.4
  6.4 101.7 %shard_map.64 = bf16[8,768,128]{2,1,0:T(8,128)(2,1)S(1)} custom-call(bf16[8,768,128]{2,1,0:T(8,128)(2,1)S(1)} %copy-done.1, bf16[3,5,2,256,128]{4,3,2,1,0:T(8,128)(2,1)S(1)} %copy-done, bf16[3,2,256,256]{3,2,1,0:T(8,128)(2,1)S(1)} %copy-done.2, bf16[1,2,64,256]{3,2,1,0:T(8,128)(2,1)S(1)} %copy-done.3, s32[3,5]{1,0:T(4,128)S(1)} %copy-done.4, ...), custom_call_target="tpu_custom_call" | custom-call | tf_op jit(solution)/shard_map/pallas_call | solution.py:293
  108.2 1.1 %copy.9 = bf16[8,768,128]{2,1,0:T(8,128)(2,1)} copy(bf16[8,768,128]{2,1,0:T(8,128)(2,1)S(1)} %shard_map.64) | data formatting | bytes 3145728
Async XLA Ops:
  0.8 1.5 %copy-start = (bf16[3,5,2,256,128]{4,3,2,1,0:T(8,128)(2,1)S(1)}, bf16[3,5,2,256,128]{4,3,2,1,0:T(8,128)(2,1)}, u32[]{:S(2)}) copy-start(bf16[3,5,2,256,128]{4,3,2,1,0:T(8,128)(2,1)} %cp.1) | copy-start | bytes 5898244
  2.4 1.4 %copy-start.1 = (bf16[8,768,128]{2,1,0:T(8,128)(2,1)S(1)}, bf16[8,768,128]{2,1,0:T(8,128)(2,1)}, u32[]{:S(2)}) copy-start(bf16[8,768,128]{2,1,0:T(8,128)(2,1)} %rs.1) | copy-start | bytes 4718596
  3.8 1.1 %copy-start.2 = (bf16[3,2,256,256]{3,2,1,0:T(8,128)(2,1)S(1)}, bf16[3,2,256,256]{3,2,1,0:T(8,128)(2,1)}, u32[]{:S(2)}) copy-start(bf16[3,2,256,256]{3,2,1,0:T(8,128)(2,1)} %di.1) | copy-start | bytes 2359300
  4.9 0.8 copy-start.3
  5.7 0.7 copy-start.4

commit v2 on v1

--- a/solution.py
+++ b/solution.py
@@ -30,9 +30,15 @@
 
 
 def kernel(
-    n, rs, cp, di, ba, nt, fb, scale, out,
-    gath, w, ds, bd, nn, y, vbuf, sbuf, gs, gr, cs, cr,
+    n, rs_in, cp_in, di_in, ba_in, nt, fb, scale, out,
+    rs, cp, di, ba, gath, w, ds, bd, nn, y, acc, vbuf, sbuf, gs, gr, cs, cr, inn, outs,
 ):
+    loads = [
+        pltpu.make_async_copy(src, dst, inn.at[k])
+        for k, (src, dst) in enumerate(((ba_in, ba), (di_in, di), (cp_in, cp), (rs_in, rs)))
+    ]
+    for load in loads:
+        load.start()
     blocks, near, _, blk, tile = cp.shape
     ticks, rows, _ = rs.shape
     rank = ba.shape[2]
@@ -44,6 +50,20 @@
     across = z * 4 + (q + 2) % 4
     beside = me + 1 - 2 * (q % 2)
 
+    def first(b):
+        return b * blk + (rank if b else 0)
+
+    def span(b):
+        return slice(first(b), first(b) + blk)
+
+    def sent(b):
+        return blk if b else blk + rank
+
+    def col(b):
+        return b * two + (2 * rank if b else 0)
+
+    extra = slice(blk, blk + rank)
+    extra_col = slice(two, two + 2 * rank)
     barrier = pltpu.get_barrier_semaphore()
 
     def greet(there, who):
@@ -125,8 +145,10 @@
         arrived(k * 4 + beside % 4)
         arrived(k * 4 + (beside + 2) % 4)
 
+    loads[0].wait()
     own_out(False)
     gath[me] = ba[0]
+    loads[1].wait()
 
     offset = lax.broadcasted_iota(jnp.int32, (blk, blk), 0) - lax.broadcasted_iota(
         jnp.int32, (blk, blk), 1
@@ -150,8 +172,13 @@
             for p in range(2):
                 piece = cp[b, place, p].astype(F32) * keep
                 nn[p * blk : (p + 1) * blk, j * tile : (j + 1) * tile] = piece.astype(BF16)
-        w[b * two : (b + 1) * two, 0:rows] = mul(ds[b], nn[...]).astype(BF16)
-
+        whole = mul(ds[b], nn[...]).astype(BF16)
+        for i in range(blocks):
+            at = slice(i * blk, (i + 1) * blk)
+            w[span(b), col(i) : col(i) + blk] = whole[0:blk, at]
+            w[span(b), col(i) + blk : col(i) + two] = whole[blk:two, at]
+
+    loads[2].wait()
     near_block(0)
     for k in range(1, blocks):
         line(k, False)
@@ -172,9 +199,10 @@
     def side_tick(t, carry):
         for b in range(blocks):
             piece = rs[t, b * blk : (b + 1) * blk, :]
-            y[t, b * blk : (b + 1) * blk, :] = complex_sum(mul(ds[b, :, 0:blk], piece))
-        return carry
-
+            y[t, span(b), :] = complex_sum(mul(ds[b, :, 0:blk], piece))
+        return carry
+
+    loads[3].wait()
     lax.fori_loop(0, ticks, side_tick, 0)
 
     def others_loop(k, carry):
@@ -183,88 +211,134 @@
 
     lax.fori_loop(0, depth, others_loop, 0)
 
-    total = jnp.zeros((2 * rank, rows + rank), F32)
     for b in range(blocks):
-        far = jnp.concatenate([gath[fb[b, 1], 0], gath[fb[b, 1], 1]], axis=1)
-        spread = lax.dot_general(
-            ds[b], far, (((1,), (1,)), ((), ())), preferred_element_type=F32
-        )
-        w[b * two : (b + 1) * two, rows : rows + rank] = (spread * scale[0]).astype(BF16)
         real, imag = gath[fb[b, 0], 0], gath[fb[b, 0], 1]
-        both = jnp.concatenate(
-            [
-                jnp.concatenate([real, -imag], axis=1),
-                jnp.concatenate([imag, real], axis=1),
-            ],
-            axis=0,
-        )
-        total = total + mul(both, w[b * two : (b + 1) * two, :])
-        bd[b] = mul(both, ds[b, :, 0:blk]).astype(BF16)
-    w[blocks * two : blocks * two + 2 * rank, :] = total.astype(BF16)
-
-    def gain_tick(t, carry):
-        gain = jnp.zeros((2 * rank, rs.shape[2]), F32)
+        bd[b, :, 0:two] = jnp.concatenate([real, -imag], axis=1)
+        low = jnp.concatenate([imag, real], axis=1)
+        both = jnp.concatenate([bd[b, :, 0:two], low], axis=0)
+        pair = mul(both, ds[b, :, 0:blk]).astype(BF16)
+        bd[b, :, two : two + blk] = pair[0:rank]
+        bd[b, :, two + blk : 2 * two] = pair[rank : 2 * rank]
+
+    def gain(t):
+        real = jnp.zeros((rank, rs.shape[2]), F32)
+        imag = jnp.zeros((rank, rs.shape[2]), F32)
         for b in range(blocks):
-            gain = gain + mul(bd[b], rs[t, b * blk : (b + 1) * blk, :])
-        y[t, rows : rows + rank, :] = complex_sum(gain)
-        return carry
-
-    lax.fori_loop(0, ticks, gain_tick, 0)
-
-    @pl.when(me == 0)
-    def _():
-        vbuf[...] = jnp.zeros_like(vbuf)
+            piece = rs[t, b * blk : (b + 1) * blk, :]
+            real = real + mul(bd[b, :, two : two + blk], piece)
+            imag = imag + mul(bd[b, :, two + blk : 2 * two], piece)
+        y[t, extra, :] = real + turned(imag)
 
     def chain_copy(t, c):
-        first = c * blk
-        count = blk if c < blocks else rank
+        at = pl.ds(first(c), sent(c))
         return pltpu.make_async_remote_copy(
-            src_ref=sbuf.at[t, pl.ds(first, count)],
-            dst_ref=vbuf.at[t, pl.ds(first, count)],
+            src_ref=sbuf.at[t, at],
+            dst_ref=vbuf.at[t, at],
             send_sem=cs.at[t, c],
             recv_sem=cr.at[t, c],
             device_id={"slab": me + 1},
             device_id_type=MESH,
         )
 
-    def tick(t, carry):
-        @pl.when(me > 0)
+    def out_copy(t, c):
+        return pltpu.make_async_copy(
+            sbuf.at[t, pl.ds(first(c), blk)], out.at[t, pl.ds(c * blk, blk)], outs.at[t, c]
+        )
+
+    def give(t, c, values):
+        sbuf[t, first(c) : first(c) + sent(c), :] = values.astype(BF16)
+
+        @pl.when(me < n - 1)
         def _():
-            for c in range(blocks + 1):
+            chain_copy(t, c).start()
+
+        out_copy(t, c).start()
+
+    @pl.when(me == 0)
+    def _():
+        def tick(t, carry):
+            gain(t)
+            for b in range(blocks):
+                give(t, b, y[t, first(b) : first(b) + sent(b), :])
+            return carry
+
+        lax.fori_loop(0, ticks, tick, 0)
+
+    @pl.when(me > 0)
+    def _():
+        for b in range(blocks):
+            real, imag = gath[fb[b, 1], 0], gath[fb[b, 1], 1]
+            far = jnp.concatenate(
+                [
+                    jnp.concatenate([real, imag], axis=1),
+                    jnp.concatenate([imag, -real], axis=1),
+                ],
+                axis=0,
+            )
+            spread = lax.dot_general(
+                ds[b, 0:blk, :], far, (((1,), (1,)), ((), ())), preferred_element_type=F32
+            )
+            w[span(b), extra_col] = (spread * scale[0]).astype(BF16)
+
+        for i in range(blocks):
+            total = jnp.zeros((2 * rank, blk), F32)
+            for b in range(blocks):
+                up = bd[b, :, 0:two]
+                down = jnp.concatenate([-up[:, blk:two], up[:, 0:blk]], axis=1)
+                stack = jnp.concatenate(
+                    [w[span(b), col(i) : col(i) + blk], w[span(b), col(i) + blk : col(i) + two]],
+                    axis=0,
+                )
+                total = total + mul(jnp.concatenate([up, down], axis=0), stack)
+            w[extra, col(i) : col(i) + blk] = total[0:rank].astype(BF16)
+            w[extra, col(i) + blk : col(i) + two] = total[rank : 2 * rank].astype(BF16)
+        total = jnp.zeros((rank, 2 * rank), F32)
+        for b in range(blocks):
+            spread = w[span(b), extra_col]
+            swapped = turned(spread.astype(F32)).astype(BF16)
+            total = total + mul(bd[b, :, 0:blk], spread) - mul(bd[b, :, blk:two], swapped)
+        w[extra, extra_col] = total.astype(BF16)
+
+        def gain_tick(t, carry):
+            gain(t)
+            return carry
+
+        lax.fori_loop(0, ticks, gain_tick, 0)
+
+        def tick(t, carry):
+            for c in range(blocks):
                 chain_copy(t, c).wait_recv()
-
-        state = vbuf[t]
-        for b in range(blocks):
-            part = slice(b * blk, (b + 1) * blk)
-            solved = y[t, part, :] - complex_sum(mul(w[b * two : (b + 1) * two, :], state))
-            solved = solved.astype(BF16)
-            out[t, part, :] = solved
-            sbuf[t, part, :] = solved
+                piece = vbuf[t, span(c), :]
+                parts = [piece, turned(piece.astype(F32)).astype(BF16)]
+                if c == 0:
+                    field = vbuf[t, extra, :].astype(F32)
+                    parts += [field.astype(BF16), turned(field).astype(BF16)]
+                state = jnp.concatenate(parts, axis=0)
+                cols = slice(col(c), col(c) + state.shape[0])
+                if c < blocks - 1:
+                    old = y[t] if c == 0 else acc[...]
+                    acc[...] = old - mul(w[:, cols], state)
+                    if c == 0:
+                        acc[extra, :] = acc[extra, :] + field
+                else:
+                    for b in range(blocks):
+                        at = slice(first(b), first(b) + sent(b))
+                        give(t, b, acc[at, :] - mul(w[at, cols], state))
+            return carry
+
+        lax.fori_loop(0, ticks, tick, 0)
+
+    def chain_end(t, carry):
+        for c in range(blocks):
+            out_copy(t, c).wait()
 
             @pl.when(me < n - 1)
             def _():
-                chain_copy(t, b).start()
-
-        part = slice(rows, rows + rank)
-        gained = y[t, part, :] - complex_sum(mul(w[blocks * two :, :], state))
-        sbuf[t, part, :] = (vbuf[t, part, :].astype(F32) + gained).astype(BF16)
-
-        @pl.when(me < n - 1)
-        def _():
-            chain_copy(t, blocks).start()
-
-        return carry
-
-    lax.fori_loop(0, ticks, tick, 0)
-
-    def chain_end(t, carry):
-        for c in range(blocks + 1):
-            chain_copy(t, c).wait_send()
-        return carry
-
-    @pl.when(me < n - 1)
-    def _():
-        lax.fori_loop(0, ticks, chain_end, 0)
+                chain_copy(t, c).wait_send()
+
+        return carry
+
+    lax.fori_loop(0, ticks, chain_end, 0)
 
     own_out(True)
 
@@ -288,29 +362,36 @@
     n = lax.axis_size("slab")
     earlier = blocks * jnp.maximum(lax.axis_index("slab"), 1)
     scale = (1.0 / jnp.sqrt(earlier.astype(F32))).reshape(1)
-    vmem = pl.BlockSpec(memory_space=pltpu.VMEM)
+    anywhere = pl.BlockSpec(memory_space=pl.ANY)
     smem = pl.BlockSpec(memory_space=pltpu.SMEM)
     return pl.pallas_call(
         functools.partial(kernel, n),
         out_shape=jax.ShapeDtypeStruct(right_side.shape, right_side.dtype),
-        in_specs=[vmem] * 4 + [smem] * 3,
-        out_specs=vmem,
+        in_specs=[anywhere] * 4 + [smem] * 3,
+        out_specs=anywhere,
         scratch_shapes=[
+            pltpu.VMEM(right_side.shape, BF16),
+            pltpu.VMEM(coupling.shape, BF16),
+            pltpu.VMEM(diag_inverse.shape, BF16),
+            pltpu.VMEM(basis.shape, BF16),
             pltpu.VMEM((n,) + basis.shape[1:], BF16),
-            pltpu.VMEM((2 * (rows + rank), rows + rank), BF16),
+            pltpu.VMEM((rows + rank, 2 * (rows + rank)), BF16),
             pltpu.VMEM((blocks, 2 * blk, 2 * blk), BF16),
-            pltpu.VMEM((blocks, 2 * rank, blk), BF16),
+            pltpu.VMEM((blocks, rank, 4 * blk), BF16),
             pltpu.VMEM((2 * blk, rows), BF16),
             pltpu.VMEM((ticks, rows + rank, columns), F32),
+            pltpu.VMEM((rows + rank, columns), F32),
             pltpu.VMEM((ticks, rows + rank, columns), BF16),
             pltpu.VMEM((ticks, rows + rank, columns), BF16),
             pltpu.SemaphoreType.DMA((4, n)),
             pltpu.SemaphoreType.DMA((n,)),
-            pltpu.SemaphoreType.DMA((ticks, blocks + 1)),
-            pltpu.SemaphoreType.DMA((ticks, blocks + 1)),
+            pltpu.SemaphoreType.DMA((ticks, blocks)),
+            pltpu.SemaphoreType.DMA((ticks, blocks)),
+            pltpu.SemaphoreType.DMA((4,)),
+            pltpu.SemaphoreType.DMA((ticks, blocks)),
         ],
         compiler_params=pltpu.CompilerParams(
-            collective_id=0, has_side_effects=True, vmem_limit_bytes=48 * 1024 * 1024
+            collective_id=0, has_side_effects=True, vmem_limit_bytes=60 * 1024 * 1024
         ),
     )(right_side, coupling, diag_inverse, basis, near_tiles, far_basis, scale)
 

time: 110 us -> 96.4 us (0.88)
  Pallas kernels: 102 us -> 92.2 us
  local copies, waits for them, and re-layouts: 7.52 us -> 4 us
    pallas_call x1, Pallas kernels: 102 us -> 92.2 us  [body(): pl.pallas_call(functools.partial(kernel, n), out_shape=jax.ShapeDtypeStru...]
    unnamed x12 -> x2, local copies, waits for them, and re-layouts: 7.52 us -> 4 us
where the time goes in v2:
time: 96.4 us; the launch traced here: 96.2 us
  Pallas kernels  92.2 us (96%)
  local copies, waits for them, and re-layouts  4 us (4%)
    pallas_call x1, Pallas kernels, body(): pl.pallas_call(functools.partial(kernel, n), out_shape=jax.ShapeDtypeStru...  92.2 us
    unnamed x2, local copies, waits for them, and re-layouts  4 us

profile of v2, /device:TPU:29, one launch (start us, length us, event | category | flops | bytes accessed | tf_op | source)
XLA Modules:
  0.0 96.2 jit_solution(11344194537693951973)
XLA Ops:
  0.0 1.3 %copy.7.fb = s32[3,2]{1,0:T(4,128)} copy(s32[3,2]{0,1:T(2,128)} %param.11) | data formatting | bytes 48 | tf_op args[5]
  1.4 92.2 %shard_map.64 = bf16[8,768,128]{2,1,0:T(8,128)(2,1)} custom-call(bf16[8,768,128]{2,1,0:T(8,128)(2,1)} %rs_in.1, bf16[3,5,2,256,128]{4,3,2,1,0:T(8,128)(2,1)} %cp_in.1, bf16[3,2,256,256]{3,2,1,0:T(8,128)(2,1)} %di_in.1, bf16[1,2,64,256]{3,2,1,0:T(8,128)(2,1)} %ba_in.1, s32[3,5]{1,0:T(4,128)} %nt.1, s32[3,2]{1,0:T(4,128)} %copy.7.fb, f32[1]{0:T(128)} %bitcast.scale), custom_call_target="tpu_custom_call" | custom-call | tf_op jit(solution)/shard_map/pallas_call | solution.py:367
  93.5 2.7 %copy.9 = bf16[8,768,128]{2,1,0:T(8,128)(2,1)} copy(bf16[8,768,128]{2,1,0:T(8,128)(2,1)} %shard_map.64) | data formatting | bytes 3145728

commit v3 on v2

--- a/solution.py
+++ b/solution.py
@@ -35,12 +35,18 @@
 ):
     loads = [
         pltpu.make_async_copy(src, dst, inn.at[k])
-        for k, (src, dst) in enumerate(((ba_in, ba), (di_in, di), (cp_in, cp), (rs_in, rs)))
+        for k, (src, dst) in enumerate(((ba_in, ba), (di_in, di), (cp_in, cp)))
+    ] + [
+        pltpu.make_async_copy(
+            rs_in.at[t], rs.at[:, pl.ds(t * rs_in.shape[2], rs_in.shape[2])], inn.at[3 + t]
+        )
+        for t in range(rs_in.shape[0])
     ]
     for load in loads:
         load.start()
     blocks, near, _, blk, tile = cp.shape
-    ticks, rows, _ = rs.shape
+    ticks, rows, columns = rs_in.shape
+    batch = 4 if ticks % 4 == 0 else 1
     rank = ba.shape[2]
     tiles = rows // tile
     two = 2 * blk
@@ -196,14 +202,14 @@
 
     lax.fori_loop(0, depth, other_loop, 0)
 
-    def side_tick(t, carry):
+    for load in loads[3:]:
+        load.wait()
+    for t in range(0, ticks, batch):
+        wide = slice(t * columns, (t + batch) * columns)
         for b in range(blocks):
-            piece = rs[t, b * blk : (b + 1) * blk, :]
-            y[t, span(b), :] = complex_sum(mul(ds[b, :, 0:blk], piece))
-        return carry
-
-    loads[3].wait()
-    lax.fori_loop(0, ticks, side_tick, 0)
+            both = mul(ds[b, :, 0:blk], rs[b * blk : (b + 1) * blk, wide])
+            for k in range(batch):
+                y[t + k, span(b), :] = complex_sum(both[:, k * columns : (k + 1) * columns])
 
     def others_loop(k, carry):
         others_in(k)
@@ -220,14 +226,16 @@
         bd[b, :, two : two + blk] = pair[0:rank]
         bd[b, :, two + blk : 2 * two] = pair[rank : 2 * rank]
 
-    def gain(t):
-        real = jnp.zeros((rank, rs.shape[2]), F32)
-        imag = jnp.zeros((rank, rs.shape[2]), F32)
+    for t in range(0, ticks, batch):
+        wide = slice(t * columns, (t + batch) * columns)
+        both = jnp.zeros((2 * rank, batch * columns), F32)
         for b in range(blocks):
-            piece = rs[t, b * blk : (b + 1) * blk, :]
-            real = real + mul(bd[b, :, two : two + blk], piece)
-            imag = imag + mul(bd[b, :, two + blk : 2 * two], piece)
-        y[t, extra, :] = real + turned(imag)
+            pair = jnp.concatenate(
+                [bd[b, :, two : two + blk], bd[b, :, two + blk : 2 * two]], axis=0
+            )
+            both = both + mul(pair, rs[b * blk : (b + 1) * blk, wide])
+        for k in range(batch):
+            y[t + k, extra, :] = complex_sum(both[:, k * columns : (k + 1) * columns])
 
     def chain_copy(t, c):
         at = pl.ds(first(c), sent(c))
@@ -257,7 +265,6 @@
     @pl.when(me == 0)
     def _():
         def tick(t, carry):
-            gain(t)
             for b in range(blocks):
                 give(t, b, y[t, first(b) : first(b) + sent(b), :])
             return carry
@@ -298,12 +305,6 @@
             swapped = turned(spread.astype(F32)).astype(BF16)
             total = total + mul(bd[b, :, 0:blk], spread) - mul(bd[b, :, blk:two], swapped)
         w[extra, extra_col] = total.astype(BF16)
-
-        def gain_tick(t, carry):
-            gain(t)
-            return carry
-
-        lax.fori_loop(0, ticks, gain_tick, 0)
 
         def tick(t, carry):
             for c in range(blocks):
@@ -370,7 +371,7 @@
         in_specs=[anywhere] * 4 + [smem] * 3,
         out_specs=anywhere,
         scratch_shapes=[
-            pltpu.VMEM(right_side.shape, BF16),
+            pltpu.VMEM((rows, ticks * columns), BF16),
             pltpu.VMEM(coupling.shape, BF16),
             pltpu.VMEM(diag_inverse.shape, BF16),
             pltpu.VMEM(basis.shape, BF16),
@@ -387,7 +388,7 @@
             pltpu.SemaphoreType.DMA((n,)),
             pltpu.SemaphoreType.DMA((ticks, blocks)),
             pltpu.SemaphoreType.DMA((ticks, blocks)),
-            pltpu.SemaphoreType.DMA((4,)),
+            pltpu.SemaphoreType.DMA((3 + ticks,)),
             pltpu.SemaphoreType.DMA((ticks, blocks)),
         ],
         compiler_params=pltpu.CompilerParams(

time: 96.4 us -> 94.2 us (0.977)
  Pallas kernels: 92.2 us -> 90 us
    pallas_call x1, Pallas kernels: 92.2 us -> 90 us  [body(): pl.pallas_call(functools.partial(kernel, n), out_shape=jax.ShapeDtypeStru...]
where the time goes in v3:
time: 94.2 us; the launch traced here: 94 us
  Pallas kernels  90 us (96%)
  local copies, waits for them, and re-layouts  4 us (4%)
    pallas_call x1, Pallas kernels, body(): pl.pallas_call(functools.partial(kernel, n), out_shape=jax.ShapeDtypeStru...  90 us
    unnamed x2, local copies, waits for them, and re-layouts  4 us

profile of v3, /device:TPU:29, one launch (start us, length us, event | category | flops | bytes accessed | tf_op | source)
XLA Modules:
  0.0 94.0 jit_solution(14269676980704971447)
XLA Ops:
  0.0 1.3 %copy.7.fb = s32[3,2]{1,0:T(4,128)} copy(s32[3,2]{0,1:T(2,128)} %param.11) | data formatting | bytes 48 | tf_op args[5]
  1.4 90.0 %shard_map.64 = bf16[8,768,128]{2,1,0:T(8,128)(2,1)} custom-call(bf16[8,768,128]{2,1,0:T(8,128)(2,1)} %rs_in.1, bf16[3,5,2,256,128]{4,3,2,1,0:T(8,128)(2,1)} %cp_in.1, bf16[3,2,256,256]{3,2,1,0:T(8,128)(2,1)} %di_in.1, bf16[1,2,64,256]{3,2,1,0:T(8,128)(2,1)} %ba_in.1, s32[3,5]{1,0:T(4,128)} %nt.1, s32[3,2]{1,0:T(4,128)} %copy.7.fb, f32[1]{0:T(128)} %bitcast.scale), custom_call_target="tpu_custom_call" | custom-call | tf_op jit(solution)/shard_map/pallas_call | solution.py:368
  91.4 2.7 %copy.9 = bf16[8,768,128]{2,1,0:T(8,128)(2,1)} copy(bf16[8,768,128]{2,1,0:T(8,128)(2,1)} %shard_map.64) | data formatting | bytes 3145728

commit v4 on v3

--- a/solution.py
+++ b/solution.py
@@ -306,25 +306,28 @@
             total = total + mul(bd[b, :, 0:blk], spread) - mul(bd[b, :, blk:two], swapped)
         w[extra, extra_col] = total.astype(BF16)
 
+        def piece(t, c):
+            own = vbuf[t, span(c), :]
+            parts = [own, turned(own.astype(F32)).astype(BF16)]
+            if c == 0:
+                field = vbuf[t, extra, :]
+                parts += [field, turned(field.astype(F32)).astype(BF16)]
+            return parts
+
+        last = col(blocks - 1)
+
         def tick(t, carry):
-            for c in range(blocks):
+            parts = []
+            for c in range(blocks - 1):
                 chain_copy(t, c).wait_recv()
-                piece = vbuf[t, span(c), :]
-                parts = [piece, turned(piece.astype(F32)).astype(BF16)]
-                if c == 0:
-                    field = vbuf[t, extra, :].astype(F32)
-                    parts += [field.astype(BF16), turned(field).astype(BF16)]
-                state = jnp.concatenate(parts, axis=0)
-                cols = slice(col(c), col(c) + state.shape[0])
-                if c < blocks - 1:
-                    old = y[t] if c == 0 else acc[...]
-                    acc[...] = old - mul(w[:, cols], state)
-                    if c == 0:
-                        acc[extra, :] = acc[extra, :] + field
-                else:
-                    for b in range(blocks):
-                        at = slice(first(b), first(b) + sent(b))
-                        give(t, b, acc[at, :] - mul(w[at, cols], state))
+                parts += piece(t, c)
+            acc[...] = y[t] - mul(w[:, 0:last], jnp.concatenate(parts, axis=0))
+            acc[extra, :] = acc[extra, :] + vbuf[t, extra, :].astype(F32)
+            chain_copy(t, blocks - 1).wait_recv()
+            tail = jnp.concatenate(piece(t, blocks - 1), axis=0)
+            done = acc[...] - mul(w[:, last : last + two], tail)
+            for b in range(blocks):
+                give(t, b, done[first(b) : first(b) + sent(b), :])
             return carry
 
         lax.fori_loop(0, ticks, tick, 0)

time: 94.2 us -> 95.3 us (1.012)
  Pallas kernels: 90 us -> 91.1 us
    pallas_call x1, Pallas kernels: 90 us -> 91.1 us  [body(): pl.pallas_call(functools.partial(kernel, n), out_shape=jax.ShapeDtypeStru...]
where the time goes in v4:
time: 95.3 us; the launch traced here: 95.1 us
  Pallas kernels  91.1 us (96%)
  local copies, waits for them, and re-layouts  4 us (4%)
    pallas_call x1, Pallas kernels, body(): pl.pallas_call(functools.partial(kernel, n), out_shape=jax.ShapeDtypeStru...  91.1 us
    unnamed x2, local copies, waits for them, and re-layouts  4 us

profile of v4, /device:TPU:29, one launch (start us, length us, event | category | flops | bytes accessed | tf_op | source)
XLA Modules:
  0.0 95.1 jit_solution(11227752589587353660)
XLA Ops:
  0.0 1.3 %copy.7.fb = s32[3,2]{1,0:T(4,128)} copy(s32[3,2]{0,1:T(2,128)} %param.11) | data formatting | bytes 48 | tf_op args[5]
  1.4 91.1 %shard_map.64 = bf16[8,768,128]{2,1,0:T(8,128)(2,1)} custom-call(bf16[8,768,128]{2,1,0:T(8,128)(2,1)} %rs_in.1, bf16[3,5,2,256,128]{4,3,2,1,0:T(8,128)(2,1)} %cp_in.1, bf16[3,2,256,256]{3,2,1,0:T(8,128)(2,1)} %di_in.1, bf16[1,2,64,256]{3,2,1,0:T(8,128)(2,1)} %ba_in.1, s32[3,5]{1,0:T(4,128)} %nt.1, s32[3,2]{1,0:T(4,128)} %copy.7.fb, f32[1]{0:T(128)} %bitcast.scale), custom_call_target="tpu_custom_call" | custom-call | tf_op jit(solution)/shard_map/pallas_call | solution.py:371
  92.4 2.7 %copy.9 = bf16[8,768,128]{2,1,0:T(8,128)(2,1)} copy(bf16[8,768,128]{2,1,0:T(8,128)(2,1)} %shard_map.64) | data formatting | bytes 3145728
